TPU v7x, 512 devices: a whole 4x8x8 slice. The times are simulated.
512 devices in a mesh: tm: 16 (over x, z_hi, core), contact: 32 (over z_lo, y).
Axes of the slice: x: 4, y: 8, z: 8 (z_hi: 2, z_lo: 4; z = z_hi * 4 + z_lo), core: 2. Of those that a mesh axis runs over, the one named last changes fastest.
Arguments:
- signal: bfloat16 [8, 512, 16384], P(None, 'contact', 'tm'), may hold values from -6 to 6
- fir_taps: bfloat16 [512, 129], P('contact'), may hold values from -0.5 to 0.5
- neighbours: int32 [512, 4], replicated, may hold values from 0 to 511, as said below
- live_mask: int32 [512], replicated, may hold values 0 or 1
- lap_coef: float32 [512], replicated, may hold values from 0.1 to 1
- w_query: bfloat16 [256, 256], replicated, may hold values from -8 to 8
- w_key: bfloat16 [256, 256], replicated, may hold values from -8 to 8
- w_value: bfloat16 [256, 256], replicated, may hold values from -0.375 to 0.375
- w_out: bfloat16 [256, 256], replicated, may hold values from -0.375 to 0.375
- cotangent: bfloat16 [8, 512, 16384], P(None, 'contact', 'tm'), may hold values from -6 to 6
Outputs:
- attended: bfloat16 [8, 512, 16384], P(None, 'contact', 'tm')
- weight_grads: float32 [4, 256, 256], replicated
Inputs may be any that keep to these rules, and one draw needn't show every extreme that they name: `neighbours`: entry [c, k] names a contact whose grid row (index // 16) differs from that of contact c by at most one and whose column (index % 16) differs by at most two.
All inputs are finite; a program needn't handle non-finite values.
Results may differ from a plain program's by a relative error of at most 0.011.
Values may be sent and summed in bfloat16 or wider, within the bound.
A program may use at most 64 MiB of HBM per device.

v0:
```python
import jax
import jax.numpy as jnp
from jax import lax
from jax.sharding import PartitionSpec as P

GRID_COLS = 16
HEADS = 4


def from_behind(value, axis, by):
    count = lax.axis_size(axis)
    pairs = [(i, i + by) for i in range(count) if 0 <= i + by < count]
    return lax.ppermute(value, axis, pairs)


def extended_2(cells, sides, width):
    for axis, dim in sides:
        count = lax.axis_size(axis)
        ends = count - 1
        head = lax.slice_in_dim(cells, 0, width, axis=dim)
        tail = lax.slice_in_dim(cells, cells.shape[dim] - width, cells.shape[dim], axis=dim)
        cells = jnp.concatenate(
            [
                lax.ppermute(tail, axis, [(i, (i + 1) % count) for i in range(ends)]),
                cells,
                lax.ppermute(head, axis, [((i + 1) % count, i) for i in range(ends)]),
            ],
            axis=dim,
        )
    return cells


def contract(left, right, left_dim, right_dim):
    return lax.dot_general(
        left, right, (((left_dim,), (right_dim,)), ((), ())), preferred_element_type=jnp.float32
    )


def toeplitz(fir_taps):
    rim_width = fir_taps.shape[1] - 1
    source = jnp.arange(2 * rim_width, dtype=jnp.int32)[:, None]
    target = jnp.arange(rim_width, dtype=jnp.int32)[None, :]
    lag_table = target + rim_width - source
    inside = (lag_table >= 0) & (lag_table <= rim_width)
    picked = jnp.take(fir_taps, jnp.clip(lag_table, 0, rim_width), axis=1)
    return jnp.where(inside[None, :, :], picked, jnp.zeros_like(picked))


def laplace(field, centre, indices, nbr_alive, own_alive, coef):
    source_ids = jnp.arange(field.shape[-2], dtype=jnp.int32)
    counts = jnp.zeros((indices.shape[0], field.shape[-2]), jnp.float32)
    for slot_index in range(indices.shape[1]):
        hit = (indices[:, slot_index][:, None] == source_ids[None, :]).astype(jnp.float32)
        counts = counts + nbr_alive[:, slot_index][:, None] * hit
    alive_count = jnp.sum(nbr_alive, axis=1)
    beside = jnp.einsum(
        "cn,bnt->bct", counts.astype(jnp.bfloat16), field, preferred_element_type=jnp.float32
    )
    middle = centre.astype(jnp.float32)
    running = beside - alive_count[:, None] * middle
    return (own_alive[:, None] * (middle + coef[:, None] * running)).astype(jnp.bfloat16)


def one_head(query_head, key_head, value_head, back_head, key_alive, score_scale):
    scores = contract(query_head, key_head, 1, 1) * score_scale
    scores = jnp.where(key_alive[None, :] > 0, scores, -1e30)
    top_score = jnp.max(scores, axis=1, keepdims=True)
    raised = jnp.exp(scores - top_score)
    attn_prob = raised / jnp.sum(raised, axis=1, keepdims=True)
    prob_low = attn_prob.astype(jnp.bfloat16)
    head_out = jnp.dot(prob_low, value_head, preferred_element_type=jnp.float32).astype(
        jnp.bfloat16
    )
    grad_value = contract(prob_low, back_head, 0, 0).astype(jnp.bfloat16)
    grad_prob = contract(back_head, value_head, 1, 1)
    row_inner = jnp.sum(
        back_head.astype(jnp.float32) * head_out.astype(jnp.float32), axis=1, keepdims=True
    )
    grad_score = (attn_prob * (grad_prob - row_inner) * score_scale).astype(jnp.bfloat16)
    grad_query = jnp.dot(grad_score, key_head, preferred_element_type=jnp.float32).astype(
        jnp.bfloat16
    )
    grad_key = contract(grad_score, query_head, 0, 0).astype(jnp.bfloat16)
    return (head_out, grad_query, grad_key, grad_value)


def group_step(tokens, upstream, key_alive, w_query, w_key, w_value, w_out):
    as_float = tokens.astype(jnp.float32)
    normed = (
        as_float * lax.rsqrt(jnp.mean(as_float * as_float, axis=1, keepdims=True) + 1e-05)
    ).astype(jnp.bfloat16)
    query_rows = jnp.dot(normed, w_query, preferred_element_type=jnp.float32).astype(jnp.bfloat16)
    key_rows = jnp.dot(normed, w_key, preferred_element_type=jnp.float32).astype(jnp.bfloat16)
    value_rows = jnp.dot(normed, w_value, preferred_element_type=jnp.float32).astype(jnp.bfloat16)
    back_signal = contract(upstream, w_out, 1, 1).astype(jnp.bfloat16)
    head_size = w_query.shape[1] // HEADS
    score_scale = head_size ** (-0.5)
    head_results = []
    for head_index in range(HEADS):
        lower = head_index * head_size
        upper = lower + head_size
        head_results.append(
            one_head(
                query_rows[:, lower:upper],
                key_rows[:, lower:upper],
                value_rows[:, lower:upper],
                back_signal[:, lower:upper],
                key_alive,
                score_scale,
            )
        )
    mixed_heads = jnp.concatenate([entry[0] for entry in head_results], axis=1)
    grad_query = jnp.concatenate([entry[1] for entry in head_results], axis=1)
    grad_key = jnp.concatenate([entry[2] for entry in head_results], axis=1)
    grad_value = jnp.concatenate([entry[3] for entry in head_results], axis=1)
    attended = jnp.dot(mixed_heads, w_out, preferred_element_type=jnp.float32).astype(jnp.bfloat16)
    grad_stack = jnp.stack(
        [
            contract(normed, grad_query, 0, 0),
            contract(normed, grad_key, 0, 0),
            contract(normed, grad_value, 0, 0),
            contract(mixed_heads, upstream, 0, 0),
        ]
    )
    return (attended, grad_stack)


def to_groups(whole, patch_len):
    batch_size, contacts_here, slab_len = whole.shape
    patch_count = slab_len // patch_len
    shaped = whole.reshape(batch_size, contacts_here, patch_count, patch_len).transpose(0, 2, 1, 3)
    return shaped.reshape(batch_size * patch_count, contacts_here, patch_len)


def from_groups(grouped, batch_size):
    group_count, contacts_here, patch_len = grouped.shape
    patch_count = group_count // batch_size
    shaped = grouped.reshape(batch_size, patch_count, contacts_here, patch_len).transpose(
        0, 2, 1, 3
    )
    return shaped.reshape(batch_size, contacts_here, patch_count * patch_len)


def local(
    signal, fir_taps, neighbours, live_mask, lap_coef, w_query, w_key, w_value, w_out, cotangent
):
    batch_size, contacts_here, slab_len = signal.shape
    rim_width = fir_taps.shape[1] - 1
    patch_len = w_query.shape[0]
    patch_count = slab_len // patch_len
    prior_rim = from_behind(signal[:, :, slab_len - rim_width :], "tm", 1)
    extended = jnp.concatenate([prior_rim, signal], axis=2)
    blocks = extended.reshape(batch_size, contacts_here, slab_len // rim_width + 1, rim_width)
    windows = jnp.concatenate([blocks[:, :, :-1], blocks[:, :, 1:]], axis=3)
    filter_table = toeplitz(fir_taps)
    filtered = jnp.einsum(
        "bcjw,cwu->bcju", windows, filter_table, preferred_element_type=jnp.float32
    )
    filtered = filtered.reshape(batch_size, contacts_here, slab_len).astype(jnp.bfloat16)
    alive_f = live_mask.astype(jnp.float32)
    nbr_alive = jnp.take(alive_f, neighbours)
    first_contact = lax.axis_index("contact") * contacts_here
    padded = extended_2(filtered, (("contact", 1),), GRID_COLS)
    local_index = (
        lax.dynamic_slice_in_dim(neighbours, first_contact, contacts_here, 0)
        - first_contact
        + GRID_COLS
    )
    ready = laplace(
        padded,
        filtered,
        local_index,
        lax.dynamic_slice_in_dim(nbr_alive, first_contact, contacts_here, 0),
        lax.dynamic_slice_in_dim(alive_f, first_contact, contacts_here, 0),
        lax.dynamic_slice_in_dim(lap_coef, first_contact, contacts_here, 0),
    )
    grouped = to_groups(ready, patch_len)
    features, upstream = (
        lax.all_to_all(grouped, "contact", split_axis=0, concat_axis=1, tiled=True),
        lax.all_to_all(
            to_groups(cotangent, patch_len), "contact", split_axis=0, concat_axis=1, tiled=True
        ),
    )

    def run_group(running, inputs_pair):
        attended, grad_stack = group_step(
            inputs_pair[0], inputs_pair[1], alive_f, w_query, w_key, w_value, w_out
        )
        return (running + grad_stack, attended)

    running, attended_groups = lax.scan(
        run_group, jnp.zeros((4, patch_len, patch_len), jnp.float32), (features, upstream)
    )
    summed = lax.psum(running, ("tm", "contact"))
    returned = lax.all_to_all(attended_groups, "contact", split_axis=1, concat_axis=0, tiled=True)
    attended = from_groups(returned, batch_size)
    grad_scale = (batch_size * patch_count * lax.axis_size("tm") * neighbours.shape[0]) ** (-0.5)
    return (attended, summed * grad_scale)


def solution(mesh):
    in_specs = (
        P(None, "contact", "tm"),
        P("contact", None),
        P(),
        P(),
        P(),
        P(),
        P(),
        P(),
        P(),
        P(None, "contact", "tm"),
    )
    out_specs = (P(None, "contact", "tm"), P())
    return jax.shard_map(local, mesh=mesh, in_specs=in_specs, out_specs=out_specs, check_vma=False)
```

profile of v0, /device:TPU:24, one launch (start us, length us, event | category | flops | bytes accessed | tf_op | source)
XLA Modules:
  0.0 490.5 jit_solution(11078941743470237049)
XLA Ops:
  7.2 0.8 slice.121
  8.0 1.7 collective-permute-start
  9.7 1.0 fusion.132
  10.7 0.7 pad_maximum_fusion.5
  11.4 12.9 %all-to-all-start.2 = ((bf16[32,16,256]{2,1,0:T(8,128)(2,1)}), bf16[32,16,256]{2,1,0:T(8,128)(2,1)S(1)}, u32[]{:S(2)}, u32[]{:S(2)}) async-start(bf16[32,16,256]{2,1,0:T(8,128)(2,1)} %bitcast.20), calls=%async_computation.2 | async-start | bytes 524288 | tf_op jit(solution)/shard_map/all_to_all | solution.py:180
  24.9 13.2 %gather_fusion.1 = f32[2048]{0:T(1024)S(1)} fusion(f32[512]{0:T(512)S(1)} %convert_element_type.188, s32[2048]{0:T(1024)S(1)} %broadcast_clamp_fusion), kind=kCustom, calls=%fused_computation.1 | custom fusion | bytes 24576 | tf_op jit(solution)/shard_map/jit(_take)/gather | solution.py:161
  38.7 114.2 %gather_fusion = bf16[32768,16]{1,0:T(8,128)(2,1)} fusion(bf16[16,129]{0,1:T(8,128)(2,1)S(1)} %copy.116, s32[32768]{0:T(1024)S(1)} %fusion.71), kind=kCustom, calls=%fused_computation | custom fusion | bytes 2228224 | tf_op jit(solution)/shard_map/jit(_take)/gather | solution.py:45
  152.9 6.9 %copy.117 = bf16[256,128,16]{1,0,2:T(8,128)(2,1)S(1)} copy(bf16[256,128,16]{2,1,0:T(8,128)(2,1)} %bitcast.104) | data formatting | bytes 2097152 | tf_op jit(solution)/shard_map/jit(_take)/gather | solution.py:45
  160.8 2.5 collective-permute-start.2
  163.3 4.6 collective-permute-start.1
  168.0 0.8 dynamic_slice.18
  168.8 1.5 collective-permute-done.2
  170.3 1.5 collective-permute-done.1
  172.1 0.7 pad_maximum_fusion.3
  172.9 11.1 %all-to-all-start = ((bf16[32,16,256]{2,1,0:T(8,128)(2,1)}), bf16[32,16,256]{2,1,0:T(8,128)(2,1)S(1)}, u32[]{:S(2)}, u32[]{:S(2)}) async-start(bf16[32,16,256]{2,1,0:T(8,128)(2,1)} %bitcast.16), calls=%async_computation | async-start | bytes 524288 | tf_op jit(solution)/shard_map/all_to_all | solution.py:179
  184.5 9.0 %all-to-all-done = bf16[32,16,256]{2,1,0:T(8,128)(2,1)S(1)} async-done(((bf16[32,16,256]{2,1,0:T(8,128)(2,1)}), bf16[32,16,256]{2,1,0:T(8,128)(2,1)S(1)}, u32[]{:S(2)}, u32[]{:S(2)}) %all-to-all-start) | async-done | bytes 262176 | tf_op jit(solution)/shard_map/all_to_all | solution.py:179
  196.3 0.5 copy-done.4
  204.9 1.0 pad_maximum_fusion
  206.7 0.5 broadcast.198
  207.2 2.2 reduce.4
  209.5 15.4 %all_to_all.12 = bf16[32,2,2048]{2,1,0:T(2,128)(2,1)S(1)} all-to-all(bf16[32,2,2048]{2,1,0:T(2,128)(2,1)S(1)} %reshape.193), channel_id=1, replica_groups=mesh['tm'=16,'contact'=32] {'contact'}, dimensions={0} | all-to-all | bytes 524288 | tf_op jit(solution)/shard_map/all_to_all | solution.py:195
  225.2 0.7 copy.142
  226.0 255.4 %all-reduce.2.cloned.1.call-done = f32[4,256,256]{2,1,0:T(8,128)} async-done(((f32[4,256,256]{2,1,0:T(8,128)}), f32[4,256,256]{2,1,0:T(8,128)}) %all-reduce.2.cloned.1.call-update) | async-done | bytes 1048592 | tf_op jit(solution)/shard_map/psum | solution.py:194
  481.4 2.3 broadcast_multiply_fusion
  (94 shorter events, 14.8 us)
Async XLA Ops:
  7.2 177.1 %copy-start = (bf16[256,256]{1,0:T(8,128)(2,1)S(1)}, bf16[256,256]{1,0:T(8,128)(2,1)}, u32[]{:S(2)}) copy-start(bf16[256,256]{1,0:T(8,128)(2,1)} %param.18) | copy-start | bytes 393220
  7.2 17.3 %copy-start.6 = (s32[512]{0:T(512)S(1)}, s32[512]{0:T(512)}, u32[]{:S(2)}) copy-start(s32[512]{0:T(512)} %param.13) | copy-start | bytes 6148
  7.2 17.3 %copy-start.5 = (s32[512,4]{0,1:T(4,128)S(1)}, s32[512,4]{0,1:T(4,128)}, u32[]{:S(2)}) copy-start(s32[512,4]{0,1:T(4,128)} %param.12) | copy-start | bytes 24580
  8.0 151.8 %collective-permute-start = (bf16[8,16,128]{2,1,0:T(8,128)(2,1)S(1)}, bf16[8,16,128]{2,1,0:T(8,128)(2,1)S(1)}, u32[]{:S(2)}, u32[]{:S(2)}) collective-permute-start(bf16[8,16,128]{2,1,0:T(8,128)(2,1)S(1)} %slice.121), channel_id=1, source_target_pairs={{0,32},{32,64},{64,96},{96,128},{128,160},{160,192},{192,224},{224... | collective-permute-start | bytes 98312 | tf_op jit(solution)/shard_map/ppermute | solution.py:13
  11.4 161.4 %all-to-all-start.2 = ((bf16[32,16,256]{2,1,0:T(8,128)(2,1)}), bf16[32,16,256]{2,1,0:T(8,128)(2,1)S(1)}, u32[]{:S(2)}, u32[]{:S(2)}) async-start(bf16[32,16,256]{2,1,0:T(8,128)(2,1)} %bitcast.20), calls=%async_computation.2 | async-start | bytes 524288 | tf_op jit(solution)/shard_map/all_to_all | solution.py:180
  24.9 13.7 %copy-start.7 = (bf16[16,129]{1,0:T(8,128)(2,1)S(1)}, bf16[16,129]{1,0:T(8,128)(2,1)}, u32[]{:S(2)}) copy-start(bf16[16,129]{1,0:T(8,128)(2,1)} %param.11) | copy-start | bytes 12388
  152.9 6.9 %copy-start.1 = (bf16[8,16,1024]{2,1,0:T(8,128)(2,1)S(1)}, bf16[8,16,1024]{2,1,0:T(8,128)(2,1)}, u32[]{:S(2)}) copy-start(bf16[8,16,1024]{2,1,0:T(8,128)(2,1)} %param.10) | copy-start | bytes 786436
  160.8 9.5 %collective-permute-start.2 = (bf16[8,16,1024]{2,1,0:T(8,128)(2,1)S(1)}, bf16[8,16,1024]{2,1,0:T(8,128)(2,1)S(1)}, u32[]{:S(2)}, u32[]{:S(2)}) collective-permute-start(bf16[8,16,1024]{2,1,0:T(8,128)(2,1)S(1)} %copy.120), channel_id=1, source_target_pairs={{1,0},{2,1},{3,2},{4,3},{5,4},{6,5},{7,6},{8,7},{9,8},{10,9},{11,1... | collective-permute-start | bytes 786440 | tf_op jit(solution)/shard_map/ppermute | solution.py:26
  163.3 8.5 %collective-permute-start.1 = (bf16[8,16,1024]{2,1,0:T(8,128)(2,1)S(1)}, bf16[8,16,1024]{2,1,0:T(8,128)(2,1)S(1)}, u32[]{:S(2)}, u32[]{:S(2)}) collective-permute-start(bf16[8,16,1024]{2,1,0:T(8,128)(2,1)S(1)} %copy.120), channel_id=1, source_target_pairs={{0,1},{1,2},{2,3},{3,4},{4,5},{5,6},{6,7},{7,8},{8,9},{9,10},{10,1... | collective-permute-start | bytes 786440 | tf_op jit(solution)/shard_map/ppermute | solution.py:24
  172.1 21.8 %copy-start.2 = (bf16[256,256]{1,0:T(8,128)(2,1)S(1)}, bf16[256,256]{1,0:T(8,128)(2,1)}, u32[]{:S(2)}) copy-start(bf16[256,256]{1,0:T(8,128)(2,1)} %param.16) | copy-start | bytes 393220
  172.1 22.1 %copy-start.3 = (bf16[256,256]{1,0:T(8,128)(2,1)S(1)}, bf16[256,256]{1,0:T(8,128)(2,1)}, u32[]{:S(2)}) copy-start(bf16[256,256]{1,0:T(8,128)(2,1)} %param.15) | copy-start | bytes 393220
  172.9 20.7 %all-to-all-start = ((bf16[32,16,256]{2,1,0:T(8,128)(2,1)}), bf16[32,16,256]{2,1,0:T(8,128)(2,1)S(1)}, u32[]{:S(2)}, u32[]{:S(2)}) async-start(bf16[32,16,256]{2,1,0:T(8,128)(2,1)} %bitcast.16), calls=%async_computation | async-start | bytes 524288 | tf_op jit(solution)/shard_map/all_to_all | solution.py:179
  184.0 297.3 %all-reduce.2.cloned.1.call-start = ((), (), s32[]{:S(2)}) async-start(), calls=%async_computation.3 | async-start | bytes 2097152 | tf_op jit(solution)/shard_map/psum | solution.py:194
  196.0 0.9 copy-start.4
Sparse Core Ops, SparseCore 0:
  206.1 275.1 all-reduce.1
where the time goes:
time: 491 us; the launch traced here: 490 us
  waiting for transfers between devices  267 us (54%)
  local copies, waits for them, and re-layouts  141 us (29%)
  starting transfers between devices  33 us (7%)
  blocking collectives  15.4 us (3%)
  between operations  14.6 us (3%)
  matrix products  10.1 us (2%)
  other arithmetic  9.12 us (2%)
    psum x1, waiting for transfers between devices, local(): summed = lax.psum(running, ('tm', 'contact'))  255 us
    gather x2, local copies, waits for them, and re-layouts, toeplitz(): picked = jnp.take(fir_taps, jnp.clip(lag_table, 0, rim_width), axis=1)  121 us
    all_to_all x1, blocking collectives, local(): lax.all_to_all(attended_groups, 'contact', split_axis=1, concat_axis=0, t...  15.4 us
    gather x2, local copies, waits for them, and re-layouts, local(): nbr_alive = jnp.take(alive_f, neighbours)  13.5 us
    all_to_all x1, starting transfers between devices, local(): lax.all_to_all(to_groups(cotangent, patch_len), 'contact', split_axis=0,...  12.9 us
    all_to_all x1, starting transfers between devices, local(): lax.all_to_all(grouped, 'contact', split_axis=0, concat_axis=1, tiled=True)  11.1 us
  transfers between devices with their start and end apart: 6, of which 4 were waited for; matrix products, arithmetic and copies ran while one was open for 30% of the time, Pallas kernels for 0%

commit v1 on v0

--- a/solution.py
+++ b/solution.py
@@ -191,7 +191,8 @@
     running, attended_groups = lax.scan(
         run_group, jnp.zeros((4, patch_len, patch_len), jnp.float32), (features, upstream)
     )
-    summed = lax.psum(running, ("tm", "contact"))
+    one_axis = lax.psum(running, "contact")
+    summed = lax.psum(one_axis, "tm")
     returned = lax.all_to_all(attended_groups, "contact", split_axis=1, concat_axis=0, tiled=True)
     attended = from_groups(returned, batch_size)
     grad_scale = (batch_size * patch_count * lax.axis_size("tm") * neighbours.shape[0]) ** (-0.5)

time: 491 us -> 713 us (1.45)
  the two profiles are of different devices: /device:TPU:24 before, /device:TPU:1 now
where the time goes in v1:
time: 713 us; the launch traced here: 712 us
  waiting for transfers between devices  483 us (68%)
  local copies, waits for them, and re-layouts  141 us (20%)
  starting transfers between devices  39 us (5%)
  blocking collectives  15.4 us (2%)
  between operations  14.6 us (2%)
  matrix products  10.1 us (1%)
  other arithmetic  9.12 us (1%)
    psum x1, waiting for transfers between devices, local(): one_axis = lax.psum(running, 'contact')  283 us
    psum x1, waiting for transfers between devices, local(): summed = lax.psum(one_axis, 'tm')  188 us
    gather x2, local copies, waits for them, and re-layouts, toeplitz(): picked = jnp.take(fir_taps, jnp.clip(lag_table, 0, rim_width), axis=1)  121 us
    all_to_all x1, blocking collectives, local(): lax.all_to_all(attended_groups, 'contact', split_axis=1, concat_axis=0, t...  15.4 us
  transfers between devices with their start and end apart: 7, of which 5 were waited for; matrix products, arithmetic and copies ran while one was open for 20% of the time, Pallas kernels for 0%

profile of v1, /device:TPU:1, one launch (start us, length us, event | category | flops | bytes accessed | tf_op | source)
XLA Modules:
  0.0 712.4 jit_solution(993340102872763163)
XLA Ops:
  7.2 0.8 slice.121
  8.0 12.0 %collective-permute-start = (bf16[8,16,128]{2,1,0:T(8,128)(2,1)S(1)}, bf16[8,16,128]{2,1,0:T(8,128)(2,1)S(1)}, u32[]{:S(2)}, u32[]{:S(2)}) collective-permute-start(bf16[8,16,128]{2,1,0:T(8,128)(2,1)S(1)} %slice.121), channel_id=1, source_target_pairs={{0,32},{32,64},{64,96},{96,128},{128,160},{160,192},{192,224},{224... | collective-permute-start | bytes 98312 | tf_op jit(solution)/shard_map/ppermute | solution.py:13
  20.0 1.0 fusion.132
  21.0 0.7 pad_maximum_fusion.5
  21.7 9.9 %all-to-all-start.2 = ((bf16[32,16,256]{2,1,0:T(8,128)(2,1)}), bf16[32,16,256]{2,1,0:T(8,128)(2,1)S(1)}, u32[]{:S(2)}, u32[]{:S(2)}) async-start(bf16[32,16,256]{2,1,0:T(8,128)(2,1)} %bitcast.20), calls=%async_computation.2 | async-start | bytes 524288 | tf_op jit(solution)/shard_map/all_to_all | solution.py:180
  32.2 13.2 %gather_fusion.1 = f32[2048]{0:T(1024)S(1)} fusion(f32[512]{0:T(512)S(1)} %convert_element_type.188, s32[2048]{0:T(1024)S(1)} %broadcast_clamp_fusion), kind=kCustom, calls=%fused_computation.1 | custom fusion | bytes 24576 | tf_op jit(solution)/shard_map/jit(_take)/gather | solution.py:161
  46.0 114.2 %gather_fusion = bf16[32768,16]{1,0:T(8,128)(2,1)} fusion(bf16[16,129]{0,1:T(8,128)(2,1)S(1)} %copy.116, s32[32768]{0:T(1024)S(1)} %fusion.71), kind=kCustom, calls=%fused_computation | custom fusion | bytes 2228224 | tf_op jit(solution)/shard_map/jit(_take)/gather | solution.py:45
  160.2 6.9 copy.117
  168.1 1.3 collective-permute-start.2
  169.4 4.0 collective-permute-start.1
  173.6 0.8 dynamic_slice.18
  174.3 0.9 collective-permute-done.2
  175.2 1.5 collective-permute-done.1
  177.1 0.7 pad_maximum_fusion.3
  177.8 11.5 %all-to-all-start = ((bf16[32,16,256]{2,1,0:T(8,128)(2,1)}), bf16[32,16,256]{2,1,0:T(8,128)(2,1)S(1)}, u32[]{:S(2)}, u32[]{:S(2)}) async-start(bf16[32,16,256]{2,1,0:T(8,128)(2,1)} %bitcast.16), calls=%async_computation | async-start | bytes 524288 | tf_op jit(solution)/shard_map/all_to_all | solution.py:179
  189.7 9.7 %all-to-all-done = bf16[32,16,256]{2,1,0:T(8,128)(2,1)S(1)} async-done(((bf16[32,16,256]{2,1,0:T(8,128)(2,1)}), bf16[32,16,256]{2,1,0:T(8,128)(2,1)S(1)}, u32[]{:S(2)}, u32[]{:S(2)}) %all-to-all-start) | async-done | bytes 262176 | tf_op jit(solution)/shard_map/all_to_all | solution.py:179
  202.2 0.5 copy-done.4
  210.8 1.0 pad_maximum_fusion
  212.1 283.4 %all-reduce.3.cloned.1.call-done = f32[4,256,256]{2,1,0:T(8,128)} async-done(((f32[4,256,256]{2,1,0:T(8,128)}), f32[4,256,256]{2,1,0:T(8,128)}) %all-reduce.3.cloned.1.call-update) | async-done | bytes 1048592 | tf_op jit(solution)/shard_map/psum | solution.py:194
  496.7 2.2 reduce.4
  499.0 15.4 %all_to_all.12 = bf16[32,2,2048]{2,1,0:T(2,128)(2,1)S(1)} all-to-all(bf16[32,2,2048]{2,1,0:T(2,128)(2,1)S(1)} %reshape.193), channel_id=1, replica_groups=mesh['tm'=16,'contact'=32] {'contact'}, dimensions={0} | all-to-all | bytes 524288 | tf_op jit(solution)/shard_map/all_to_all | solution.py:196
  514.7 0.7 copy.142
  515.4 187.9 %all-reduce.5.cloned.1.call-done = f32[4,256,256]{2,1,0:T(8,128)} async-done(((f32[4,256,256]{2,1,0:T(8,128)}), f32[4,256,256]{2,1,0:T(8,128)}) %all-reduce.5.cloned.1.call-update) | async-done | bytes 1048592 | tf_op jit(solution)/shard_map/psum | solution.py:195
  703.3 2.3 broadcast_multiply_fusion
  (97 shorter events, 15.3 us)
Async XLA Ops:
  7.2 182.2 %copy-start = (bf16[256,256]{1,0:T(8,128)(2,1)S(1)}, bf16[256,256]{1,0:T(8,128)(2,1)}, u32[]{:S(2)}) copy-start(bf16[256,256]{1,0:T(8,128)(2,1)} %param.18) | copy-start | bytes 393220
  7.2 24.7 %copy-start.6 = (s32[512]{0:T(512)S(1)}, s32[512]{0:T(512)}, u32[]{:S(2)}) copy-start(s32[512]{0:T(512)} %param.13) | copy-start | bytes 6148
  7.2 24.7 %copy-start.5 = (s32[512,4]{0,1:T(4,128)S(1)}, s32[512,4]{0,1:T(4,128)}, u32[]{:S(2)}) copy-start(s32[512,4]{0,1:T(4,128)} %param.12) | copy-start | bytes 24580
  8.0 159.1 %collective-permute-start = (bf16[8,16,128]{2,1,0:T(8,128)(2,1)S(1)}, bf16[8,16,128]{2,1,0:T(8,128)(2,1)S(1)}, u32[]{:S(2)}, u32[]{:S(2)}) collective-permute-start(bf16[8,16,128]{2,1,0:T(8,128)(2,1)S(1)} %slice.121), channel_id=1, source_target_pairs={{0,32},{32,64},{64,96},{96,128},{128,160},{160,192},{192,224},{224... | collective-permute-start | bytes 98312 | tf_op jit(solution)/shard_map/ppermute | solution.py:13
  21.7 156.1 %all-to-all-start.2 = ((bf16[32,16,256]{2,1,0:T(8,128)(2,1)}), bf16[32,16,256]{2,1,0:T(8,128)(2,1)S(1)}, u32[]{:S(2)}, u32[]{:S(2)}) async-start(bf16[32,16,256]{2,1,0:T(8,128)(2,1)} %bitcast.20), calls=%async_computation.2 | async-start | bytes 524288 | tf_op jit(solution)/shard_map/all_to_all | solution.py:180
  32.2 13.7 %copy-start.7 = (bf16[16,129]{1,0:T(8,128)(2,1)S(1)}, bf16[16,129]{1,0:T(8,128)(2,1)}, u32[]{:S(2)}) copy-start(bf16[16,129]{1,0:T(8,128)(2,1)} %param.11) | copy-start | bytes 12388
  160.2 6.9 copy-start.1
  168.1 7.1 collective-permute-start.2
  169.4 7.3 %collective-permute-start.1 = (bf16[8,16,1024]{2,1,0:T(8,128)(2,1)S(1)}, bf16[8,16,1024]{2,1,0:T(8,128)(2,1)S(1)}, u32[]{:S(2)}, u32[]{:S(2)}) collective-permute-start(bf16[8,16,1024]{2,1,0:T(8,128)(2,1)S(1)} %copy.120), channel_id=1, source_target_pairs={{0,1},{1,2},{2,3},{3,4},{4,5},{5,6},{6,7},{7,8},{8,9},{9,10},{10,1... | collective-permute-start | bytes 786440 | tf_op jit(solution)/shard_map/ppermute | solution.py:24
  177.0 22.7 %copy-start.2 = (bf16[256,256]{1,0:T(8,128)(2,1)S(1)}, bf16[256,256]{1,0:T(8,128)(2,1)}, u32[]{:S(2)}) copy-start(bf16[256,256]{1,0:T(8,128)(2,1)} %param.16) | copy-start | bytes 393220
  177.1 23.0 %copy-start.3 = (bf16[256,256]{1,0:T(8,128)(2,1)S(1)}, bf16[256,256]{1,0:T(8,128)(2,1)}, u32[]{:S(2)}) copy-start(bf16[256,256]{1,0:T(8,128)(2,1)} %param.15) | copy-start | bytes 393220
  177.8 21.6 %all-to-all-start = ((bf16[32,16,256]{2,1,0:T(8,128)(2,1)}), bf16[32,16,256]{2,1,0:T(8,128)(2,1)S(1)}, u32[]{:S(2)}, u32[]{:S(2)}) async-start(bf16[32,16,256]{2,1,0:T(8,128)(2,1)} %bitcast.16), calls=%async_computation | async-start | bytes 524288 | tf_op jit(solution)/shard_map/all_to_all | solution.py:179
  189.3 306.2 %all-reduce.3.cloned.1.call-start = ((), (), s32[]{:S(2)}) async-start(), calls=%async_computation.3 | async-start | bytes 2097152 | tf_op jit(solution)/shard_map/psum | solution.py:194
  201.8 0.9 copy-start.4
  211.9 491.5 %all-reduce.5.cloned.1.call-start = ((), (), s32[]{:S(2)}) async-start(), calls=%async_computation.4 | async-start | bytes 2097152 | tf_op jit(solution)/shard_map/psum | solution.py:195
Sparse Core Ops, SparseCore 0:
  212.0 283.4 all-reduce.2
  498.7 204.6 all-reduce.4
